TPU v7x, 512 devices: a whole 4x4x16 slice. The times are simulated.
512 devices in a mesh: seq: 64 (over z, y), exp: 8 (over x, core).
Axes of the slice: x: 4, y: 4, z: 16, core: 2. Of those that a mesh axis runs over, the one named last changes fastest.
Arguments:
- queries: bfloat16 [16384, 6144], P('seq', 'exp'), may hold values from -6 to 6
- keys: bfloat16 [16384, 6144], P('seq', 'exp'), may hold values from -6 to 6
- values: bfloat16 [16384, 6144], P('seq', 'exp'), may hold values from -6 to 6
- selections: int32 [64, 8, 5], P('seq'), may hold values from 0 to 255
- router: bfloat16 [6144, 8], P(None, 'exp'), may hold values from -0.0390625 to 0.0390625
- w_up: bfloat16 [8, 9216, 6144], P('exp', 'seq'), may hold values from -0.15625 to 0.15625
- w_down: bfloat16 [8, 6144, 9216], P('exp', 'seq'), may hold values from -0.125 to 0.125
Outputs:
- layer_out: bfloat16 [16384, 6144], P('seq', 'exp')
Inputs may be any that keep to these rules, and one draw needn't show every extreme that they name: `selections`: entries are positions inside the block of 256 tokens; different experts may pick the same token and an expert may pick a token twice.
All inputs are finite; a program needn't handle non-finite values.
Results may differ from a plain program's by a relative error of at most 0.018.
Values may be sent and summed in bfloat16 or wider, within the bound.
No kernel may reach another device: no remote copies, remote signals or barrier semaphores. Data moves between devices by JAX's collectives and lax.ppermute only.
A program may use at most 128 MiB of HBM per device.

v0:
```python
import jax
import jax.numpy as jnp
from jax import lax
from jax.sharding import PartitionSpec as P

HEAD = 96


def entering(array, axis, join, neutral):
    place = lax.axis_index(axis)
    gathered = lax.all_gather(array.astype(jnp.bfloat16), axis)
    state = jnp.zeros_like(array) + jnp.asarray(neutral, array.dtype)

    def one(lap, state):
        return join(state, lax.dynamic_index_in_dim(gathered, lap, 0, False).astype(array.dtype))

    return lax.fori_loop(0, place, one, state)


def body(queries, keys, values, selections, router, w_up, w_down):
    length = queries.shape[0]
    width = queries.shape[1]
    heads_here = width // HEAD
    query_heads = queries.reshape(length, heads_here, HEAD)
    key_heads = keys.reshape(length, heads_here, HEAD)
    value_heads = values.reshape(length, heads_here, HEAD)
    state = jnp.einsum(
        "lhd,lhe->hde", key_heads, value_heads, preferred_element_type=jnp.float32
    ).astype(jnp.bfloat16)
    flat_size = heads_here * HEAD * HEAD
    flat_state = state.reshape(1, flat_size).astype(jnp.float32)
    empty_state = jnp.zeros((1, flat_size), jnp.float32)

    def combine_sum(earlier, later):
        return earlier + later

    before = entering(flat_state, "seq", combine_sum, empty_state)
    before = before.astype(jnp.bfloat16).reshape(heads_here, HEAD, HEAD)
    causal = jnp.arange(length)[:, None] >= jnp.arange(length)[None, :]
    scores = jnp.einsum("qhd,khd->hqk", query_heads, key_heads, preferred_element_type=jnp.float32)
    scores = jnp.where(causal[None], scores, 0.0).astype(jnp.bfloat16)
    inner = jnp.einsum("hqk,khe->qhe", scores, value_heads, preferred_element_type=jnp.float32)
    outer = jnp.einsum("qhd,hde->qhe", query_heads, before, preferred_element_type=jnp.float32)
    mixed = inner + outer
    power = jnp.mean(mixed * mixed, axis=-1, keepdims=True)
    attn = (mixed * lax.rsqrt(power + 1e-06)).astype(jnp.bfloat16).reshape(length, width)
    experts = selections.shape[1]
    capacity = selections.shape[2]
    where = selections[0].reshape(-1)
    picked = attn[where].reshape(experts, capacity, width)
    up_matrix = w_up[0]
    down_matrix = w_down[0]
    arrived = lax.all_to_all(picked, "exp", split_axis=0, concat_axis=2, tiled=True)
    own_rows = arrived.reshape(capacity, -1)
    hidden = jax.nn.silu(
        jnp.einsum(
            "rd,fd->rf",
            lax.all_gather(own_rows, "seq", axis=0, tiled=True),
            up_matrix,
            preferred_element_type=jnp.float32,
        )
    ).astype(jnp.bfloat16)
    gate_value = jax.nn.sigmoid(jnp.dot(own_rows, router, preferred_element_type=jnp.float32))
    columns = jnp.einsum(
        "rf,cf->rc",
        lax.all_gather(hidden, "seq", axis=1, tiled=True),
        down_matrix,
        preferred_element_type=jnp.float32,
    )
    expert_out = lax.all_to_all(columns, "seq", split_axis=0, concat_axis=1, tiled=True)
    weighted = (gate_value * expert_out).astype(jnp.bfloat16).reshape(1, capacity, -1)
    back = lax.all_to_all(weighted, "exp", split_axis=2, concat_axis=0, tiled=True)
    placing = (where[None, :] == jnp.arange(length, dtype=jnp.int32)[:, None]).astype(jnp.bfloat16)
    added = jnp.dot(
        placing, back.reshape(experts * capacity, width), preferred_element_type=jnp.float32
    )
    return (attn.astype(jnp.float32) + added).astype(jnp.bfloat16)


def solution(mesh):
    placed = (
        P("seq", "exp"),
        P("seq", "exp"),
        P("seq", "exp"),
        P("seq", None, None),
        P(None, "exp"),
        P("exp", "seq", None),
        P("exp", "seq", None),
    )
    return jax.shard_map(
        body, mesh=mesh, in_specs=placed, out_specs=P("seq", "exp"), check_vma=False
    )
```

profile of v0, /device:TPU:1, one launch (start us, length us, event | category | flops | bytes accessed | tf_op | source)
XLA Modules:
  0.0 761.9 jit_solution(10522953082573374514)
XLA Ops:
  6.5 1.3 copy.44
  7.9 1.2 copy.45
  9.3 1.0 all_gather.12
  10.4 1.2 copy.43
  11.8 209.9 %all-gather.5.cloned.1.call-done = bf16[64,1,73728]{2,1,0:T(2,128)(2,1)} async-done(((bf16[1,1,73728]{2,1,0:T(2,128)(2,1)}), bf16[64,1,73728]{2,1,0:T(2,128)(2,1)}) %all-gather.5.cloned.1.call-update) | async-done | bytes 9437200 | tf_op jit(solution)/shard_map/all_gather | solution.py:11
  221.9 0.8 convert_reduce_fusion
  222.8 1.2 convolution_bitcast_fusion
  224.0 2.8 multiply_reduce_fusion
  226.8 1.2 multiply_convert_fusion
  228.2 0.6 gather_fusion
  228.9 10.2 %all_to_all.46 = bf16[8,5,768]{2,1,0:T(8,128)(2,1)} all-to-all(bf16[8,5,768]{2,1,0:T(8,128)(2,1)S(1)} %reshape.140), channel_id=1, replica_groups=mesh['seq'=64,'exp'=8] {'exp'}, dimensions={0} | all-to-all | bytes 122880 | tf_op jit(solution)/shard_map/all_to_all | solution.py:53
  239.4 225.6 %all-gather.9.cloned.1.call-done = bf16[64,5,6144]{2,1,0:T(8,128)(2,1)} async-done(((bf16[1,5,6144]{2,1,0:T(8,128)(2,1)}), bf16[64,5,6144]{2,1,0:T(8,128)(2,1)}) %all-gather.9.cloned.1.call-update) | async-done | bytes 3932176 | tf_op jit(solution)/shard_map/all_gather | solution.py:58
  465.0 7.7 %reshape.154 = bf16[320,6144]{1,0:T(8,128)(2,1)} reshape(bf16[64,5,6144]{2,1,0:T(8,128)(2,1)} %all-gather.9.cloned.1.call-done) | data formatting | bytes 7864320
  472.7 4.3 multiply_convert_fusion.1
  477.0 148.1 %all-gather.7.cloned.1.call-done = bf16[320,9216]{0,1:T(8,128)(2,1)} async-done(((bf16[320,144]{0,1:T(8,128)(2,1)}), bf16[320,9216]{0,1:T(8,128)(2,1)}) %all-gather.7.cloned.1.call-update) | async-done | bytes 5898256 | tf_op jit(solution)/shard_map/all_gather | solution.py:66
  625.1 9.3 %copy.51 = bf16[320,9216]{1,0:T(8,128)(2,1)} copy(bf16[320,9216]{0,1:T(8,128)(2,1)} %all-gather.7.cloned.1.call-done) | data formatting | bytes 11796480 | tf_op jit(solution)/shard_map/all_gather | solution.py:66
  634.4 9.2 %dot_general.32 = bf16[64,5,9216]{2,1,0:T(8,128)(2,1)} reshape(bf16[320,9216]{1,0:T(8,128)(2,1)} %copy.51) | data formatting | bytes 11796480 | tf_op jit(solution)/shard_map/rf,cf->rc/dot_general | solution.py:64
  643.6 10.6 %fusion = f32[64,5,96]{2,0,1:T(8,128)S(1)} fusion(bf16[64,5,9216]{2,1,0:T(8,128)(2,1)} %dot_general.32, bf16[1,96,9216]{2,1,0:T(8,128)(2,1)} %param.15), kind=kOutput, calls=%fused_computation.2 | convolution fusion | flops 566231040 | bytes 7790592 | tf_op jit(solution)/shard_map/rf,cf->rc/dot_general | solution.py:64
  654.3 0.9 reshape.161
  655.2 9.4 %all-to-all-start.1 = ((f32[64,1,480]{2,1,0:T(1,128)}), f32[64,1,480]{2,1,0:T(1,128)S(1)}, u32[]{:S(2)}, u32[]{:S(2)}) async-start(f32[64,1,480]{2,1,0:T(1,128)} %reshape.161), calls=%async_computation.1 | async-start | bytes 262144 | tf_op jit(solution)/shard_map/all_to_all | solution.py:70
  664.7 14.7 %all-to-all-done.1 = f32[64,1,480]{2,1,0:T(1,128)S(1)} async-done(((f32[64,1,480]{2,1,0:T(1,128)}), f32[64,1,480]{2,1,0:T(1,128)S(1)}, u32[]{:S(2)}, u32[]{:S(2)}) %all-to-all-start.1) | async-done | bytes 122912 | tf_op jit(solution)/shard_map/all_to_all | solution.py:70
  679.4 0.5 broadcast.59
  680.0 0.9 reduce.2
  681.3 5.2 copy.55
  686.5 0.5 broadcast.60
  687.0 34.2 %reduce.3 = bf16[6144,5]{1,0:T(8,128)(2,1)S(1)} reduce(bf16[6144,1,5]{2,1,0:T(2,128)(2,1)} %bitcast.68, bf16[]{:T(256)} %broadcast.60), dimensions={1}, to_apply=%bitcast.51.reduce_sub_computation | reduce | bytes 122882
  721.2 3.0 reshape.163
  724.3 14.1 %all-to-all-start.2 = ((bf16[8,2,1920]{2,1,0:T(2,128)(2,1)}), bf16[8,2,1920]{2,1,0:T(2,128)(2,1)S(1)}, u32[]{:S(2)}, u32[]{:S(2)}) async-start(bf16[8,2,1920]{2,1,0:T(2,128)(2,1)} %reshape.163), calls=%async_computation.2 | async-start | bytes 122880 | tf_op jit(solution)/shard_map/all_to_all | solution.py:72
  738.4 4.8 all-to-all-done.2
  743.2 5.1 reshape.164
  748.3 6.0 copy.56
  754.4 1.0 fusion.8
  (42 shorter events, 2.1 us)
Async XLA Ops:
  6.5 466.1 %copy-start = (bf16[1,144,6144]{2,1,0:T(8,128)(2,1)S(1)}, bf16[1,144,6144]{2,1,0:T(8,128)(2,1)}, u32[]{:S(2)}) copy-start(bf16[1,144,6144]{2,1,0:T(8,128)(2,1)} %param.14) | copy-start | bytes 5308420
  6.5 5.0 copy-start.5
  6.5 215.2 %all-gather.5.cloned.1.call-start = ((), (), s32[]{:S(2)}) async-start(), calls=%async_computation.3 | async-start | bytes 19169280 | tf_op jit(solution)/shard_map/all_gather | solution.py:11
  10.3 454.7 %all-gather.9.cloned.1.call-start = ((), (), s32[]{:S(2)}) async-start(), calls=%async_computation.5 | async-start | bytes 6389760 | tf_op jit(solution)/shard_map/all_gather | solution.py:58
  228.2 244.5 %copy-start.2 = (bf16[256,768]{1,0:T(8,128)(2,1)}, bf16[256,768]{1,0:T(8,128)(2,1)S(1)}, u32[]{:S(2)}) copy-start(bf16[256,768]{1,0:T(8,128)(2,1)S(1)} %copy.47) | copy-start | bytes 1179652
  239.1 386.0 %all-gather.7.cloned.1.call-start = ((), (), s32[]{:S(2)}) async-start(), calls=%async_computation.4 | async-start | bytes 7188480 | tf_op jit(solution)/shard_map/all_gather | solution.py:66
  643.6 21.0 %copy-start.4 = (bf16[8,5,768]{2,1,0:T(8,128)(2,1)S(1)}, bf16[8,5,768]{2,1,0:T(8,128)(2,1)}, u32[]{:S(2)}) copy-start(bf16[8,5,768]{2,1,0:T(8,128)(2,1)} %all_to_all.46) | copy-start | bytes 184324
  643.6 21.0 %copy-start.6 = (bf16[6144,1]{0,1:T(2,128)(2,1)S(1)}, bf16[6144,1]{0,1:T(2,128)(2,1)}, u32[]{:S(2)}) copy-start(bf16[6144,1]{0,1:T(2,128)(2,1)} %param.13) | copy-start | bytes 36868
  655.2 24.2 %all-to-all-start.1 = ((f32[64,1,480]{2,1,0:T(1,128)}), f32[64,1,480]{2,1,0:T(1,128)S(1)}, u32[]{:S(2)}, u32[]{:S(2)}) async-start(f32[64,1,480]{2,1,0:T(1,128)} %reshape.161), calls=%async_computation.1 | async-start | bytes 262144 | tf_op jit(solution)/shard_map/all_to_all | solution.py:70
  721.2 34.1 %copy-start.1 = (bf16[1,144,6144]{2,1,0:T(8,128)(2,1)S(1)}, bf16[1,144,6144]{2,1,0:T(8,128)(2,1)}, u32[]{:S(2)}) copy-start(bf16[1,144,6144]{2,1,0:T(8,128)(2,1)} %param.14) | copy-start | bytes 5308420
  724.3 30.1 %copy-start.3 = (bf16[256,768]{1,0:T(8,128)(2,1)S(1)}, bf16[256,768]{1,0:T(8,128)(2,1)}, u32[]{:S(2)}) copy-start(bf16[256,768]{1,0:T(8,128)(2,1)} %copy-done.2) | copy-start | bytes 1179652
  724.3 18.9 %all-to-all-start.2 = ((bf16[8,2,1920]{2,1,0:T(2,128)(2,1)}), bf16[8,2,1920]{2,1,0:T(2,128)(2,1)S(1)}, u32[]{:S(2)}, u32[]{:S(2)}) async-start(bf16[8,2,1920]{2,1,0:T(2,128)(2,1)} %reshape.163), calls=%async_computation.2 | async-start | bytes 122880 | tf_op jit(solution)/shard_map/all_to_all | solution.py:72
Sparse Core Ops, SparseCore 0:
  10.4 211.2 all-gather.4
  239.3 225.6 all-gather.8
  477.2 147.9 all-gather.6
where the time goes:
time: 765 us; the launch traced here: 762 us
  waiting for transfers between devices  603 us (79%)
  local copies, waits for them, and re-layouts  53.9 us (7%)
  other arithmetic  37.3 us (5%)
  starting transfers between devices  23.7 us (3%)
  matrix products  20.3 us (3%)
  between operations  13.3 us (2%)
  blocking collectives  10.2 us (1%)
    all_gather x1, waiting for transfers between devices, body(): lax.all_gather(own_rows, 'seq', axis=0, tiled=True)  226 us
    all_gather x1, waiting for transfers between devices, entering(): gathered = lax.all_gather(array.astype(jnp.bfloat16), axis)  210 us
    all_gather x1, waiting for transfers between devices, body(): lax.all_gather(hidden, 'seq', axis=1, tiled=True)  148 us
    unnamed x1, other arithmetic  34.2 us
    unnamed x25, local copies, waits for them, and re-layouts  21 us
  transfers between devices with their start and end apart: 5, of which 5 were waited for; matrix products, arithmetic and copies ran while one was open for 0% of the time, Pallas kernels for 0%

commit v1 on v0

--- a/solution.py
+++ b/solution.py
@@ -69,7 +69,10 @@
     )
     expert_out = lax.all_to_all(columns, "seq", split_axis=0, concat_axis=1, tiled=True)
     weighted = (gate_value * expert_out).astype(jnp.bfloat16).reshape(1, capacity, -1)
-    back = lax.all_to_all(weighted, "exp", split_axis=2, concat_axis=0, tiled=True)
+    back = jnp.concatenate(
+        lax.all_to_all(jnp.stack(jnp.split(weighted, lax.axis_size("exp"), axis=2)), "exp", 0, 0),
+        axis=0,
+    )
     placing = (where[None, :] == jnp.arange(length, dtype=jnp.int32)[:, None]).astype(jnp.bfloat16)
     added = jnp.dot(
         placing, back.reshape(experts * capacity, width), preferred_element_type=jnp.float32

time: 765 us -> 716 us (0.936)
  other arithmetic: 37.3 us -> 3.06 us
  local copies, waits for them, and re-layouts: 53.9 us -> 38.8 us
    unnamed x1 -> x0, other arithmetic: 34.2 us -> none
    unnamed x25 -> x22, local copies, waits for them, and re-layouts: 21 us -> 16.6 us
where the time goes in v1:
time: 716 us; the launch traced here: 713 us
  waiting for transfers between devices  604 us (84%)
  local copies, waits for them, and re-layouts  38.8 us (5%)
  starting transfers between devices  23.4 us (3%)
  matrix products  20.3 us (3%)
  between operations  13.3 us (2%)
  blocking collectives  10.2 us (1%)
    all_gather x1, waiting for transfers between devices, body(): lax.all_gather(own_rows, 'seq', axis=0, tiled=True)  226 us
    all_gather x1, waiting for transfers between devices, entering(): gathered = lax.all_gather(array.astype(jnp.bfloat16), axis)  210 us
    all_gather x1, waiting for transfers between devices, body(): lax.all_gather(hidden, 'seq', axis=1, tiled=True)  148 us
    unnamed x22, local copies, waits for them, and re-layouts  16.6 us
    all_to_all x1, waiting for transfers between devices, body(): lax.all_to_all(columns, 'seq', split_axis=0, concat_axis=1, tiled=True)  14.9 us
  transfers between devices with their start and end apart: 5, of which 5 were waited for; matrix products, arithmetic and copies ran while one was open for 0% of the time, Pallas kernels for 0%

profile of v1, /device:TPU:1, one launch (start us, length us, event | category | flops | bytes accessed | tf_op | source)
XLA Modules:
  0.0 712.6 jit_solution(10451731566077537861)
XLA Ops:
  6.5 1.3 copy.29
  7.9 1.2 copy.30
  9.3 1.0 all_gather.12
  10.4 1.2 copy.28
  11.8 209.9 %all-gather.5.cloned.1.call-done = bf16[64,1,73728]{2,1,0:T(2,128)(2,1)} async-done(((bf16[1,1,73728]{2,1,0:T(2,128)(2,1)}), bf16[64,1,73728]{2,1,0:T(2,128)(2,1)}) %all-gather.5.cloned.1.call-update) | async-done | bytes 9437200 | tf_op jit(solution)/shard_map/all_gather | solution.py:11
  221.9 0.8 convert_reduce_fusion
  222.8 1.2 convolution_bitcast_fusion
  224.0 2.8 multiply_reduce_fusion
  226.8 1.2 multiply_convert_fusion
  228.2 0.6 gather_fusion
  228.9 10.2 %all_to_all.36 = bf16[8,5,768]{2,1,0:T(8,128)(2,1)} all-to-all(bf16[8,5,768]{2,1,0:T(8,128)(2,1)S(1)} %reshape.136), channel_id=1, replica_groups=mesh['seq'=64,'exp'=8] {'exp'}, dimensions={0} | all-to-all | bytes 122880 | tf_op jit(solution)/shard_map/all_to_all | solution.py:53
  239.4 225.6 %all-gather.9.cloned.1.call-done = bf16[64,5,6144]{2,1,0:T(8,128)(2,1)} async-done(((bf16[1,5,6144]{2,1,0:T(8,128)(2,1)}), bf16[64,5,6144]{2,1,0:T(8,128)(2,1)}) %all-gather.9.cloned.1.call-update) | async-done | bytes 3932176 | tf_op jit(solution)/shard_map/all_gather | solution.py:58
  465.0 7.7 %reshape.149 = bf16[320,6144]{1,0:T(8,128)(2,1)} reshape(bf16[64,5,6144]{2,1,0:T(8,128)(2,1)} %all-gather.9.cloned.1.call-done) | data formatting | bytes 7864320
  472.7 4.3 multiply_convert_fusion.1
  477.0 148.1 %all-gather.7.cloned.1.call-done = bf16[320,9216]{0,1:T(8,128)(2,1)} async-done(((bf16[320,144]{0,1:T(8,128)(2,1)}), bf16[320,9216]{0,1:T(8,128)(2,1)}) %all-gather.7.cloned.1.call-update) | async-done | bytes 5898256 | tf_op jit(solution)/shard_map/all_gather | solution.py:66
  625.2 9.3 %copy.36 = bf16[320,9216]{1,0:T(8,128)(2,1)} copy(bf16[320,9216]{0,1:T(8,128)(2,1)} %all-gather.7.cloned.1.call-done) | data formatting | bytes 11796480 | tf_op jit(solution)/shard_map/all_gather | solution.py:66
  634.4 9.2 %dot_general.32 = bf16[64,5,9216]{2,1,0:T(8,128)(2,1)} reshape(bf16[320,9216]{1,0:T(8,128)(2,1)} %copy.36) | data formatting | bytes 11796480 | tf_op jit(solution)/shard_map/rf,cf->rc/dot_general | solution.py:64
  643.6 10.6 %fusion = f32[64,5,96]{2,0,1:T(8,128)S(1)} fusion(bf16[64,5,9216]{2,1,0:T(8,128)(2,1)} %dot_general.32, bf16[1,96,9216]{2,1,0:T(8,128)(2,1)} %param.15), kind=kOutput, calls=%fused_computation.2 | convolution fusion | flops 566231040 | bytes 7790592 | tf_op jit(solution)/shard_map/rf,cf->rc/dot_general | solution.py:64
  654.3 0.9 reshape.156
  655.2 9.1 %all-to-all-start.1 = ((f32[64,1,480]{2,1,0:T(1,128)}), f32[64,1,480]{2,1,0:T(1,128)S(1)}, u32[]{:S(2)}, u32[]{:S(2)}) async-start(f32[64,1,480]{2,1,0:T(1,128)} %reshape.156), calls=%async_computation.1 | async-start | bytes 262144 | tf_op jit(solution)/shard_map/all_to_all | solution.py:70
  664.5 14.9 %all-to-all-done.1 = f32[64,1,480]{2,1,0:T(1,128)S(1)} async-done(((f32[64,1,480]{2,1,0:T(1,128)}), f32[64,1,480]{2,1,0:T(1,128)S(1)}, u32[]{:S(2)}, u32[]{:S(2)}) %all-to-all-start.1) | async-done | bytes 122912 | tf_op jit(solution)/shard_map/all_to_all | solution.py:70
  680.0 1.0 reduce.2
  681.3 0.6 constant_dynamic-update-slice_fusion.7
  681.9 0.6 constant_dynamic-update-slice_fusion.6
  682.5 0.6 constant_dynamic-update-slice_fusion.5
  683.1 0.6 constant_dynamic-update-slice_fusion.4
  683.7 0.6 constant_dynamic-update-slice_fusion.3
  684.3 0.6 constant_dynamic-update-slice_fusion.2
  685.5 0.6 constant_dynamic-update-slice_fusion
  686.1 14.0 %all-to-all-start.2 = ((bf16[8,1,5,768]{3,2,1,0:T(8,128)(2,1)}), bf16[8,1,5,768]{3,2,1,0:T(8,128)(2,1)S(1)}, u32[]{:S(2)}, u32[]{:S(2)}) async-start(bf16[8,1,5,768]{3,2,1,0:T(8,128)(2,1)} %constant_dynamic-update-slice_fusion), calls=%async_computation.2 | async-start | bytes 196608 | tf_op jit(solution)/shard_map/all_to_all | solution.py:73
  700.1 4.9 all-to-all-done.2
  705.1 1.0 fusion.8
  (36 shorter events, 3.2 us)
Async XLA Ops:
  6.5 466.1 %copy-start = (bf16[1,144,6144]{2,1,0:T(8,128)(2,1)S(1)}, bf16[1,144,6144]{2,1,0:T(8,128)(2,1)}, u32[]{:S(2)}) copy-start(bf16[1,144,6144]{2,1,0:T(8,128)(2,1)} %param.14) | copy-start | bytes 5308420
  6.5 5.0 copy-start.2
  6.5 215.2 %all-gather.5.cloned.1.call-start = ((), (), s32[]{:S(2)}) async-start(), calls=%async_computation.3 | async-start | bytes 19169280 | tf_op jit(solution)/shard_map/all_gather | solution.py:11
  10.3 454.7 %all-gather.9.cloned.1.call-start = ((), (), s32[]{:S(2)}) async-start(), calls=%async_computation.5 | async-start | bytes 6389760 | tf_op jit(solution)/shard_map/all_gather | solution.py:58
  239.1 386.0 %all-gather.7.cloned.1.call-start = ((), (), s32[]{:S(2)}) async-start(), calls=%async_computation.4 | async-start | bytes 7188480 | tf_op jit(solution)/shard_map/all_gather | solution.py:66
  643.6 20.8 %copy-start.1 = (bf16[8,5,768]{2,1,0:T(8,128)(2,1)S(1)}, bf16[8,5,768]{2,1,0:T(8,128)(2,1)}, u32[]{:S(2)}) copy-start(bf16[8,5,768]{2,1,0:T(8,128)(2,1)} %all_to_all.36) | copy-start | bytes 184324
  643.6 20.8 %copy-start.3 = (bf16[6144,1]{0,1:T(2,128)(2,1)S(1)}, bf16[6144,1]{0,1:T(2,128)(2,1)}, u32[]{:S(2)}) copy-start(bf16[6144,1]{0,1:T(2,128)(2,1)} %param.13) | copy-start | bytes 36868
  655.2 24.2 %all-to-all-start.1 = ((f32[64,1,480]{2,1,0:T(1,128)}), f32[64,1,480]{2,1,0:T(1,128)S(1)}, u32[]{:S(2)}, u32[]{:S(2)}) async-start(f32[64,1,480]{2,1,0:T(1,128)} %reshape.156), calls=%async_computation.1 | async-start | bytes 262144 | tf_op jit(solution)/shard_map/all_to_all | solution.py:70
  686.1 18.9 %all-to-all-start.2 = ((bf16[8,1,5,768]{3,2,1,0:T(8,128)(2,1)}), bf16[8,1,5,768]{3,2,1,0:T(8,128)(2,1)S(1)}, u32[]{:S(2)}, u32[]{:S(2)}) async-start(bf16[8,1,5,768]{3,2,1,0:T(8,128)(2,1)} %constant_dynamic-update-slice_fusion), calls=%async_computation.2 | async-start | bytes 196608 | tf_op jit(solution)/shard_map/all_to_all | solution.py:73
Sparse Core Ops, SparseCore 0:
  10.4 211.2 all-gather.4
  239.2 225.6 all-gather.8
  477.2 147.9 all-gather.6
